TPU v7x, 32 devices: a whole 2x2x4 slice. The times are simulated.
32 devices in a mesh: dp: 8 (over z, y), tensor: 4 (over x, core).
Axes of the slice: x: 2, y: 2, z: 4, core: 2. Of those that a mesh axis runs over, the one named last changes fastest.
Arguments:
- tokens: bfloat16 [8192, 2048], P('dp'), may hold values from -6 to 6
- segment_ids: int32 [8, 1024], P('dp'), may hold values from 0 to 7, never falling along the last dimension, each value on 1 to 512 neighbouring positions
- attn_gain: bfloat16 [2048], P('dp'), may hold values from 0.25 to 1.75
- query_weight: bfloat16 [2048, 2048], P('dp', 'tensor'), may hold values from -0.125 to 0.125
- key_weight: bfloat16 [2048, 512], P('dp', 'tensor'), may hold values from -0.125 to 0.125
- value_weight: bfloat16 [2048, 512], P('dp', 'tensor'), may hold values from -0.125 to 0.125
- output_weight: bfloat16 [2048, 2048], P('tensor', 'dp'), may hold values from -0.5 to 0.5
- ffn_gain: bfloat16 [2048], P('dp'), may hold values from 0.25 to 1.75
- gate_weight: bfloat16 [2048, 8192], P('dp', 'tensor'), may hold values from -0.125 to 0.125
- up_weight: bfloat16 [2048, 8192], P('dp', 'tensor'), may hold values from -0.125 to 0.125
- down_weight: bfloat16 [8192, 2048], P('tensor', 'dp'), may hold values from -0.0625 to 0.0625
- cotangent: bfloat16 [8192, 2048], P('dp'), may hold values from -6 to 6
Outputs:
- layer_output: bfloat16 [8192, 2048], P('dp')
- tokens_grad: float32 [8192, 2048], P('dp')
- attn_gain_grad: float32 [2048], P('dp')
- query_weight_grad: float32 [2048, 2048], P('dp', 'tensor')
- key_weight_grad: float32 [2048, 512], P('dp', 'tensor')
- value_weight_grad: float32 [2048, 512], P('dp', 'tensor')
- output_weight_grad: float32 [2048, 2048], P('tensor', 'dp')
- ffn_gain_grad: float32 [2048], P('dp')
- gate_weight_grad: float32 [2048, 8192], P('dp', 'tensor')
- up_weight_grad: float32 [2048, 8192], P('dp', 'tensor')
- down_weight_grad: float32 [8192, 2048], P('tensor', 'dp')
Inputs may be any that keep to these rules, and one draw needn't show every extreme that they name: In each row of segment_ids the numbers never fall; each document spans 1 to 512 positions, and one spans exactly 512.
All inputs are finite; a program needn't handle non-finite values.
Results may differ from a plain program's by a relative error of at most 0.02.
Values may be sent and summed in bfloat16 or wider, within the bound.
A program may use at most 256 MiB of HBM per device.

v0:
```python
from functools import partial
import math
import jax
import jax.numpy as jnp
from jax import lax
from jax.sharding import PartitionSpec as P

HD = 64
epsilon = 1e-05


def rope_tables(segment_row, head_size):
    length = segment_row.shape[0]
    places = jnp.arange(length, dtype=jnp.int32)
    boundary = jnp.concatenate([jnp.ones((1,), dtype=bool), segment_row[1:] != segment_row[:-1]])
    starts = lax.cummax(jnp.where(boundary, places, 0), axis=0)
    position = (places - starts).astype(jnp.float32)
    half_size = head_size // 2
    exponent = jnp.arange(half_size, dtype=jnp.float32) * 2.0 / head_size
    inverse = 1.0 / 500000.0**exponent
    wavelen = 2.0 * math.pi / inverse
    smooth = (8192.0 / wavelen - 1.0) / 3.0
    scaled = jnp.where(
        wavelen < 2048.0,
        inverse,
        jnp.where(
            wavelen > 8192.0, inverse / 32.0, (1.0 - smooth) * inverse / 32.0 + smooth * inverse
        ),
    )
    angles = position[:, None] * scaled[None, :]
    cosine_table = jnp.cos(angles)
    sine_table = jnp.sin(angles)
    return (
        jnp.concatenate([cosine_table, cosine_table], axis=-1),
        jnp.concatenate([sine_table, sine_table], axis=-1),
    )


def rotate(values, cosine_table, sine_table):
    half_size = values.shape[-1] // 2
    turned = jnp.concatenate([-values[..., half_size:], values[..., :half_size]], axis=-1)
    return values * cosine_table + turned * sine_table


def rms_norm(values, gain_vector):
    factor = lax.rsqrt(jnp.mean(values * values, axis=-1, keepdims=True) + epsilon)
    return values * factor * gain_vector


def swiglu(gate_values, up_values):
    return jax.nn.silu(gate_values) * up_values


def contract_rows(left_side, right_side):
    return lax.dot_general(
        left_side, right_side, (((0,), (0,)), ((), ())), preferred_element_type=jnp.float32
    )


def contract_cols(left_side, right_side):
    return lax.dot_general(
        left_side, right_side, (((1,), (1,)), ((), ())), preferred_element_type=jnp.float32
    )


def block_scores(query_block, key_seq, segment_row, start_row):
    row_count = query_block.shape[0]
    length = key_seq.shape[0]
    score_scale = query_block.shape[-1] ** (-0.5)
    scores = (
        jnp.einsum("qkgd,skd->kgqs", query_block, key_seq, preferred_element_type=jnp.float32)
        * score_scale
    )
    row_ids = start_row + jnp.arange(row_count, dtype=jnp.int32)
    col_ids = jnp.arange(length, dtype=jnp.int32)
    same_doc = segment_row[start_row : start_row + row_count][:, None] == segment_row[None, :]
    allowed = same_doc & (col_ids[None, :] <= row_ids[:, None])
    return jnp.where(allowed, scores, -1000000000.0)


def attend_forward(operands):
    query_seq, key_seq, value_seq, segment_row = operands
    length, kv_local, head_size = key_seq.shape
    grouped = query_seq.reshape(length, kv_local, -1, head_size)
    block_rows = min(512, length)
    mixed_parts = []
    total_parts = []
    for start_row in range(0, length, block_rows):
        scores = block_scores(
            grouped[start_row : start_row + block_rows], key_seq, segment_row, start_row
        )
        row_max = jnp.max(scores, axis=-1, keepdims=True)
        log_total = jnp.log(jnp.sum(jnp.exp(scores - row_max), axis=-1, keepdims=True)) + row_max
        soft_low = jnp.exp(scores - log_total).astype(jnp.bfloat16)
        mixed_block = jnp.einsum(
            "kgqs,skd->qkgd", soft_low, value_seq, preferred_element_type=jnp.float32
        )
        mixed_parts.append(mixed_block.reshape(block_rows, -1).astype(jnp.bfloat16))
        total_parts.append(log_total)
    return (jnp.concatenate(mixed_parts, axis=0), jnp.concatenate(total_parts, axis=2))


def attend_backward(operands):
    query_seq, key_seq, value_seq, log_total, grad_seq, segment_row = operands
    length, kv_local, head_size = key_seq.shape
    grouped = query_seq.reshape(length, kv_local, -1, head_size)
    grad_grouped = grad_seq.reshape(length, kv_local, -1, head_size)
    block_rows = min(512, length)
    score_scale = head_size ** (-0.5)
    query_parts = []
    key_grad = jnp.zeros(key_seq.shape, jnp.float32)
    value_grad = jnp.zeros(value_seq.shape, jnp.float32)
    for start_row in range(0, length, block_rows):
        query_block = grouped[start_row : start_row + block_rows]
        grad_block = grad_grouped[start_row : start_row + block_rows]
        scores = block_scores(query_block, key_seq, segment_row, start_row)
        soft_weights = jnp.exp(scores - log_total[:, :, start_row : start_row + block_rows])
        soft_grad = jnp.einsum(
            "qkgd,skd->kgqs", grad_block, value_seq, preferred_element_type=jnp.float32
        )
        score_grad = (
            soft_weights * (soft_grad - jnp.sum(soft_weights * soft_grad, axis=-1, keepdims=True))
        ).astype(jnp.bfloat16)
        query_parts.append(
            jnp.einsum("kgqs,skd->qkgd", score_grad, key_seq, preferred_element_type=jnp.float32)
            * score_scale
        )
        key_grad = (
            key_grad
            + jnp.einsum(
                "kgqs,qkgd->skd", score_grad, query_block, preferred_element_type=jnp.float32
            )
            * score_scale
        )
        value_grad = value_grad + jnp.einsum(
            "kgqs,qkgd->skd",
            soft_weights.astype(jnp.bfloat16),
            grad_block,
            preferred_element_type=jnp.float32,
        )
    query_grad = jnp.concatenate(query_parts, axis=0).reshape(length, -1, head_size)
    return (query_grad, key_grad, value_grad)


def shards(
    tokens,
    segment_ids,
    attn_gain,
    query_weight,
    key_weight,
    value_weight,
    output_weight,
    ffn_gain,
    gate_weight,
    up_weight,
    down_weight,
    cotangent,
):
    gathered = (
        lax.all_gather(attn_gain, "dp", axis=0, tiled=True),
        lax.all_gather(query_weight, "dp", axis=0, tiled=True),
        lax.all_gather(key_weight, "dp", axis=0, tiled=True),
        lax.all_gather(value_weight, "dp", axis=0, tiled=True),
        lax.all_gather(output_weight, "dp", axis=1, tiled=True),
        lax.all_gather(ffn_gain, "dp", axis=0, tiled=True),
        lax.all_gather(gate_weight, "dp", axis=0, tiled=True),
        lax.all_gather(up_weight, "dp", axis=0, tiled=True),
        lax.all_gather(down_weight, "dp", axis=1, tiled=True),
    )
    seq_count, length = segment_ids.shape
    token_count = tokens.shape[0]
    tokens_float = tokens.astype(jnp.float32)
    cotangent_float = cotangent.astype(jnp.float32)
    attn_scale = gathered[0].astype(jnp.float32)
    ffn_scale = gathered[5].astype(jnp.float32)
    normed = rms_norm(tokens_float, attn_scale).astype(jnp.bfloat16)
    query_raw = jnp.dot(normed, gathered[1], preferred_element_type=jnp.float32)
    key_raw = jnp.dot(normed, gathered[2], preferred_element_type=jnp.float32)
    value_low = jnp.dot(normed, gathered[3], preferred_element_type=jnp.float32).astype(
        jnp.bfloat16
    )
    cosine_table, sine_table = jax.vmap(partial(rope_tables, head_size=HD))(segment_ids)
    cosine_wide = cosine_table[:, :, None, :]
    sine_wide = sine_table[:, :, None, :]
    query_shaped = query_raw.reshape(seq_count, length, -1, HD)
    key_shaped = key_raw.reshape(seq_count, length, -1, HD)
    query_low = rotate(query_shaped, cosine_wide, sine_wide).astype(jnp.bfloat16)
    key_low = rotate(key_shaped, cosine_wide, sine_wide).astype(jnp.bfloat16)
    value_seqs = value_low.reshape(seq_count, length, -1, HD)
    mixed_low, log_total = lax.map(attend_forward, (query_low, key_low, value_seqs, segment_ids))
    mixed_low = mixed_low.reshape(token_count, -1)
    attn_part = jnp.dot(mixed_low, gathered[4], preferred_element_type=jnp.float32)
    hidden_state = tokens_float + lax.psum(attn_part, "tensor")
    normed_two = rms_norm(hidden_state, ffn_scale).astype(jnp.bfloat16)
    gate_values = jnp.dot(normed_two, gathered[6], preferred_element_type=jnp.float32)
    up_values = jnp.dot(normed_two, gathered[7], preferred_element_type=jnp.float32)
    active = swiglu(gate_values, up_values).astype(jnp.bfloat16)
    ffn_part = jnp.dot(active, gathered[8], preferred_element_type=jnp.float32)
    layer_output = (
        hidden_state + lax.psum(ffn_part.astype(jnp.bfloat16), "tensor").astype(jnp.float32)
    ).astype(jnp.bfloat16)
    down_grad = contract_rows(active, cotangent)
    active_grad = contract_cols(cotangent, gathered[8])
    unused_value, swiglu_pull = jax.vjp(swiglu, gate_values, up_values)
    gate_grad, up_grad = swiglu_pull(active_grad)
    gate_low = gate_grad.astype(jnp.bfloat16)
    up_low = up_grad.astype(jnp.bfloat16)
    gate_weight_grad = contract_rows(normed_two, gate_low)
    up_weight_grad = contract_rows(normed_two, up_low)
    mlp_part = contract_cols(gate_low, gathered[6]) + contract_cols(up_low, gathered[7])
    normed_two_grad = lax.psum(mlp_part, "tensor")
    unused_second, second_pull = jax.vjp(rms_norm, hidden_state, ffn_scale)
    hidden_part, ffn_gain_grad = second_pull(normed_two_grad)
    hidden_grad = cotangent_float + hidden_part
    hidden_low = hidden_grad.astype(jnp.bfloat16)
    output_weight_grad = contract_rows(mixed_low, hidden_low)
    mixed_grad = contract_cols(hidden_low, gathered[4]).astype(jnp.bfloat16)
    query_grad, key_grad, value_grad = lax.map(
        attend_backward,
        (
            query_low,
            key_low,
            value_seqs,
            log_total,
            mixed_grad.reshape(seq_count, length, -1, HD),
            segment_ids,
        ),
    )
    unused_query, query_pull = jax.vjp(
        partial(rotate, cosine_table=cosine_wide, sine_table=sine_wide), query_shaped
    )
    unused_key, key_pull = jax.vjp(
        partial(rotate, cosine_table=cosine_wide, sine_table=sine_wide), key_shaped
    )
    query_raw_grad = query_pull(query_grad)[0].reshape(token_count, -1).astype(jnp.bfloat16)
    key_raw_grad = key_pull(key_grad)[0].reshape(token_count, -1).astype(jnp.bfloat16)
    value_raw_grad = value_grad.reshape(token_count, -1).astype(jnp.bfloat16)
    query_weight_grad = contract_rows(normed, query_raw_grad)
    key_weight_grad = contract_rows(normed, key_raw_grad)
    value_weight_grad = contract_rows(normed, value_raw_grad)
    attn_back_part = (
        contract_cols(query_raw_grad, gathered[1])
        + contract_cols(key_raw_grad, gathered[2])
        + contract_cols(value_raw_grad, gathered[3])
    )
    normed_grad = lax.psum(attn_back_part.astype(jnp.bfloat16), "tensor").astype(jnp.float32)
    unused_first, first_pull = jax.vjp(rms_norm, tokens_float, attn_scale)
    token_part, attn_gain_grad = first_pull(normed_grad)
    tokens_grad = hidden_grad + token_part
    summed = (
        lax.psum_scatter(
            attn_gain_grad.astype(jnp.bfloat16), "dp", scatter_dimension=0, tiled=True
        ).astype(jnp.float32),
        lax.psum_scatter(
            query_weight_grad.astype(jnp.bfloat16), "dp", scatter_dimension=0, tiled=True
        ).astype(jnp.float32),
        lax.psum_scatter(
            key_weight_grad.astype(jnp.bfloat16), "dp", scatter_dimension=0, tiled=True
        ).astype(jnp.float32),
        lax.psum_scatter(
            value_weight_grad.astype(jnp.bfloat16), "dp", scatter_dimension=0, tiled=True
        ).astype(jnp.float32),
        lax.psum_scatter(
            output_weight_grad.astype(jnp.bfloat16), "dp", scatter_dimension=1, tiled=True
        ).astype(jnp.float32),
        lax.psum_scatter(
            ffn_gain_grad.astype(jnp.bfloat16), "dp", scatter_dimension=0, tiled=True
        ).astype(jnp.float32),
        lax.psum_scatter(
            gate_weight_grad.astype(jnp.bfloat16), "dp", scatter_dimension=0, tiled=True
        ).astype(jnp.float32),
        lax.psum_scatter(
            up_weight_grad.astype(jnp.bfloat16), "dp", scatter_dimension=0, tiled=True
        ).astype(jnp.float32),
        lax.psum_scatter(
            down_grad.astype(jnp.bfloat16), "dp", scatter_dimension=1, tiled=True
        ).astype(jnp.float32),
    )
    attn_gain_total = summed[0]
    ffn_gain_total = summed[5]
    return (
        layer_output,
        tokens_grad,
        attn_gain_total,
        summed[1],
        summed[2],
        summed[3],
        summed[4],
        ffn_gain_total,
        summed[6],
        summed[7],
        summed[8],
    )


def solution(mesh):
    return jax.shard_map(
        shards,
        mesh=mesh,
        in_specs=(
            P("dp", None),
            P("dp", None),
            P("dp"),
            P("dp", "tensor"),
            P("dp", "tensor"),
            P("dp", "tensor"),
            P("tensor", "dp"),
            P("dp"),
            P("dp", "tensor"),
            P("dp", "tensor"),
            P("tensor", "dp"),
            P("dp", None),
        ),
        out_specs=(
            P("dp", None),
            P("dp", None),
            P("dp"),
            P("dp", "tensor"),
            P("dp", "tensor"),
            P("dp", "tensor"),
            P("tensor", "dp"),
            P("dp"),
            P("dp", "tensor"),
            P("dp", "tensor"),
            P("tensor", "dp"),
        ),
        check_vma=False,
    )
```

profile of v0, /device:TPU:0, one launch (start us, length us, event | category | flops | bytes accessed | tf_op | source)
XLA Modules:
  0.0 1853.7 jit_solution(15969643140244901022)
XLA Ops:
  10.9 3.1 fusion.19
  15.5 22.5 %all-gather = bf16[8,1,256]{2,1,0:T(2,128)(2,1)S(1)} all-gather(bf16[1,1,256]{2,1,0:T(2,128)(2,1)S(1)} %reshape.443), channel_id=1, replica_groups=mesh['dp'=8,'tensor'=4] {'dp'}, dimensions={0}, use_global_device_ids=true | all-gather | bytes 4608 | tf_op jit(solution)/shard_map/all_gather | solution.py:160
  38.7 33.1 %all_gather.29 = bf16[2048,128]{1,0:T(8,128)(2,1)S(1)} all-gather(bf16[256,128]{1,0:T(8,128)(2,1)} %param.16), channel_id=1, replica_groups=mesh['dp'=8,'tensor'=4] {'dp'}, dimensions={0}, use_global_device_ids=true | all-gather | bytes 589824 | tf_op jit(solution)/shard_map/all_gather | solution.py:162
  71.8 32.3 %all_gather.28 = bf16[2048,128]{1,0:T(8,128)(2,1)S(1)} all-gather(bf16[256,128]{1,0:T(8,128)(2,1)} %param.17), channel_id=1, replica_groups=mesh['dp'=8,'tensor'=4] {'dp'}, dimensions={0}, use_global_device_ids=true | all-gather | bytes 589824 | tf_op jit(solution)/shard_map/all_gather | solution.py:163
  104.2 3.4 fusion.12
  112.1 5.3 fusion.64
  118.3 7.7 fusion.11
  126.0 9.2 exponential_reduce_fusion
  135.3 7.3 fusion.10
  142.6 9.2 exponential_reduce_fusion.1
  151.8 8.4 convolution_convert_fusion.8
  160.2 2.3 copy-done
  162.5 4.1 convolution_convert_fusion.9
  166.7 7.5 fusion.41
  176.0 16.3 all-gather.1
  192.3 132.1 %all-reduce.12.cloned.1.call-done = f32[1024,2048]{1,0:T(8,128)} async-done(((f32[1024,2048]{1,0:T(8,128)}), f32[1024,2048]{1,0:T(8,128)}) %all-reduce.12.cloned.1.call-update) | async-done | bytes 8388624 | tf_op jit(solution)/shard_map/psum | solution.py:193
  324.5 5.7 multiply_reduce_fusion.2
  330.2 3.4 copy-done.1
  333.6 2.7 multiply_convert_fusion.2
  336.3 114.8 %all-gather.14.cloned.1.call-done = bf16[2048,2048]{1,0:T(8,128)(2,1)} async-done(((bf16[256,2048]{1,0:T(8,128)(2,1)}), bf16[2048,2048]{1,0:T(8,128)(2,1)}) %all-gather.14.cloned.1.call-update) | async-done | bytes 8388624 | tf_op jit(solution)/shard_map/all_gather | solution.py:167
  451.1 14.7 fusion.66
  465.8 110.0 %all-gather.12.cloned.1.call-done = bf16[2048,2048]{1,0:T(8,128)(2,1)} async-done(((bf16[256,2048]{1,0:T(8,128)(2,1)}), bf16[2048,2048]{1,0:T(8,128)(2,1)}) %all-gather.12.cloned.1.call-update) | async-done | bytes 8388624 | tf_op jit(solution)/shard_map/all_gather | solution.py:166
  575.8 14.6 fusion.65
  590.3 110.5 %all-gather.16.cloned.1.call-done = bf16[2048,2048]{1,0:T(8,128)(2,1)} async-done(((bf16[2048,256]{1,0:T(8,128)(2,1)}), bf16[2048,2048]{1,0:T(8,128)(2,1)}) %all-gather.16.cloned.1.call-update) | async-done | bytes 8388624 | tf_op jit(solution)/shard_map/all_gather | solution.py:168
  700.8 21.7 %multiply_convert_fusion = (bf16[1024,2048]{1,0:T(8,128)(2,1)}, bf16[1024,2048]{1,0:T(8,128)(2,1)}, bf16[1024,2048]{1,0:T(8,128)(2,1)}) fusion(f32[1024,2048]{1,0:T(8,128)} %fusion.65, f32[1024,2048]{1,0:T(8,128)} %fusion.66, bf16[1024,2048]{1,0:T(8,128)(2,1)} %param.23, bf16[2048,2048]{1,0:T(8,128)(2,1)} %all-gather.16.cloned.1.call-done), kind=kOutput, calls=%fused_computation.44 | convolution fusion | flops 8623489024 | bytes 41943040 | tf_op jit(solution)/shard_map/dot_general | solution.py:61
  722.5 13.1 fusion.67
  735.7 13.6 convolution_add_fusion
  751.1 149.5 %all-reduce.14.cloned.1.call-done = f32[1024,2048]{1,0:T(8,128)} async-done(((f32[1024,2048]{1,0:T(8,128)}), f32[1024,2048]{1,0:T(8,128)}) %all-reduce.14.cloned.1.call-update) | async-done | bytes 8388624 | tf_op jit(solution)/shard_map/psum | solution.py:211
  900.6 7.9 multiply_reduce_fusion
  908.5 9.6 fusion.17
  918.1 6.6 fusion.32
  925.4 5.2 convolution_bitcast_fusion
  930.6 9.4 fusion
  940.0 13.8 fusion.3
  953.8 8.6 fusion.40
  962.5 2.1 convolution_convert_fusion.6
  964.7 30.0 %fusion.2 = (bf16[2,4,512,1024]{2,3,1,0:T(8,128)(2,1)}, bf16[2,4,512,1024]{2,3,1,0:T(8,128)(2,1)}) fusion(f32[2,1024,512,4]{2,1,3,0:T(8,128)} %get-tuple-element.98, f32[2,1024,512,4]{2,1,3,0:T(8,128)} %get-tuple-element.94, f32[2,4,512]{2,1,0:T(4,128)S(1)} %copy-done.35, f32[2,4,512]{2,1,0:T(4,128)S(1)} %bitcast.237, ...), kind=kLoop, calls=%fused_computation.4 | loop fusion | flops 50331648 | bytes 85000192 | tf_op jit(solution)/shard_map/while/body/eval_jaxpr/convert_element_type | solution.py:123
  994.7 6.2 convolution_bitcast_fusion.2
  1000.9 2.6 fusion.38
  1003.8 2.1 convolution_convert_fusion.7
  1006.0 7.1 convolution_convert_fusion.4
  1013.4 5.0 fusion.35
  1018.4 5.0 fusion.36
  1025.7 3.8 convolution_convert_fusion.5
  1029.6 13.8 convolution_convert_fusion.3
  1045.0 2.4 fusion.68
  1047.4 3.3 add_convert_fusion
  1051.0 14.1 convolution_convert_fusion
  1065.2 14.1 convolution_convert_fusion.1
  1079.6 14.2 convolution_convert_fusion.2
  1098.7 66.6 %reduce-scatter.14.cloned.1.call-done = bf16[512,256]{1,0:T(8,128)(2,1)} async-done(((bf16[512,2048]{1,0:T(8,128)(2,1)}), bf16[512,256]{1,0:T(8,128)(2,1)}) %reduce-scatter.14.cloned.1.call-update) | async-done | bytes 262160 | tf_op jit(solution)/shard_map/reduce_scatter | solution.py:263
  1167.0 69.8 %reduce-scatter.8.cloned.1.call-done = bf16[256,512]{1,0:T(8,128)(2,1)} async-done(((bf16[2048,512]{1,0:T(8,128)(2,1)}), bf16[256,512]{1,0:T(8,128)(2,1)}) %reduce-scatter.8.cloned.1.call-update) | async-done | bytes 262160 | tf_op jit(solution)/shard_map/reduce_scatter | solution.py:254
  1236.8 1.8 convert_element_type.232
  1238.6 153.1 %all-reduce.16.cloned.1.call-done = (bf16[1024,2048]{1,0:T(8,128)(2,1)}, bf16[1024,2048]{1,0:T(8,128)(2,1)}) async-done(((bf16[1024,2048]{1,0:T(8,128)(2,1)}, bf16[1024,2048]{1,0:T(8,128)(2,1)}), (bf16[1024,2048]{1,0:T(8,128)(2,1)}, bf16[1024,2048]{1,0:T(8,128)(2,1)})) %all-reduce.16.cloned.1.call-update) | async-done | bytes 8388624 | tf_op jit(solution)/shard_map/psum | solution.py:200
  1391.7 5.9 fusion.13
  1397.7 22.9 %all-reduce.6 = (bf16[2048]{0:T(1024)(128)(2,1)S(1)}, bf16[2048]{0:T(1024)(128)(2,1)S(1)}) all-reduce(bf16[2048]{0:T(1024)(128)(2,1)S(1)} %get-tuple-element.54, bf16[2048]{0:T(1024)(128)(2,1)S(1)} %copy-done.41), channel_id=2, replica_groups=mesh['dp'=8,'tensor'=4] {'dp'}, use_global_device_ids=true, to_apply=%region_17.18.clone | all-reduce | flops 4096 | bytes 16384
  1421.9 8.6 add_convert_fusion.1
  1430.5 6.9 fusion.18
  1437.4 106.4 %reduce-scatter.20.cloned.1.call-done = bf16[2048,256]{1,0:T(8,128)(2,1)} async-done(((bf16[2048,2048]{1,0:T(8,128)(2,1)}), bf16[2048,256]{1,0:T(8,128)(2,1)}) %reduce-scatter.20.cloned.1.call-update) | async-done | bytes 1048592 | tf_op jit(solution)/shard_map/reduce_scatter | solution.py:275
  1543.8 2.7 convert_element_type.246
  1546.5 147.4 %reduce-scatter.18.cloned.1.call-done = bf16[256,2048]{1,0:T(8,128)(2,1)} async-done(((bf16[2048,2048]{1,0:T(8,128)(2,1)}), bf16[256,2048]{1,0:T(8,128)(2,1)}) %reduce-scatter.18.cloned.1.call-update) | async-done | bytes 1048592 | tf_op jit(solution)/shard_map/reduce_scatter | solution.py:272
  1693.9 2.8 convert_element_type.244
  1696.7 147.3 %reduce-scatter.16.cloned.1.call-done = bf16[256,2048]{1,0:T(8,128)(2,1)} async-done(((bf16[2048,2048]{1,0:T(8,128)(2,1)}), bf16[256,2048]{1,0:T(8,128)(2,1)}) %reduce-scatter.16.cloned.1.call-update) | async-done | bytes 1048592 | tf_op jit(solution)/shard_map/reduce_scatter | solution.py:269
  1844.0 2.8 convert_element_type.242
  (194 shorter events, 27.7 us)
Async XLA Ops:
  7.2 104.9 %all-gather.8.cloned.1.call-start = ((), (), s32[]{:S(2)}) async-start(), calls=%async_computation.7 | async-start | bytes 2359296 | tf_op jit(solution)/shard_map/all_gather | solution.py:161
  7.9 158.7 %all-gather.10.cloned.1.call-start = ((), (), s32[]{:S(2)}) async-start(), calls=%async_computation.8 | async-start | bytes 2359296 | tf_op jit(solution)/shard_map/all_gather | solution.py:164
  8.7 315.8 %all-reduce.12.cloned.1.call-start = ((), (), s32[]{:S(2)}) async-start(), calls=%async_computation.9 | async-start | bytes 16777216 | tf_op jit(solution)/shard_map/psum | solution.py:193
  14.6 96.5 %copy-start.37 = (f32[1024]{0:T(1024)}, f32[1024]{0:T(1024)S(1)}, u32[]{:S(2)}) copy-start(f32[1024]{0:T(1024)S(1)} %fusion.50) | copy-start | bytes 12292
  38.0 73.1 %copy-start.33 = (f32[8,1,256]{2,1,0:T(1,128)}, f32[8,1,256]{2,1,0:T(1,128)S(1)}, u32[]{:S(2)}) copy-start(f32[8,1,256]{2,1,0:T(1,128)S(1)} %convert_element_type.247) | copy-start | bytes 24580
  38.6 65.6 %copy-start.26 = (f32[1,1024,32]{1,2,0:T(8,128)}, f32[1,1024,32]{1,2,0:T(8,128)S(1)}, u32[]{:S(2)}) copy-start(f32[1,1024,32]{1,2,0:T(8,128)S(1)} %get-tuple-element.87) | copy-start | bytes 393220
  38.6 65.6 %copy-start.28 = (f32[1,1024,32]{1,2,0:T(8,128)}, f32[1,1024,32]{1,2,0:T(8,128)S(1)}, u32[]{:S(2)}) copy-start(f32[1,1024,32]{1,2,0:T(8,128)S(1)} %get-tuple-element.88) | copy-start | bytes 393220
  38.6 79.0 %copy-start.24 = (f32[1024,64]{0,1:T(8,128)}, f32[1024,64]{0,1:T(8,128)S(1)}, u32[]{:S(2)}) copy-start(f32[1024,64]{0,1:T(8,128)S(1)} %maximum_bitcast_fusion) | copy-start | bytes 786436
  38.7 78.9 %copy-start.22 = (f32[1024,64]{0,1:T(8,128)}, f32[1024,64]{0,1:T(8,128)S(1)}, u32[]{:S(2)}) copy-start(f32[1024,64]{0,1:T(8,128)S(1)} %maximum_bitcast_fusion.1) | copy-start | bytes 786436
  71.8 39.3 %copy-start.15 = (bf16[2048,128]{1,0:T(8,128)(2,1)}, bf16[2048,128]{1,0:T(8,128)(2,1)S(1)}, u32[]{:S(2)}) copy-start(bf16[2048,128]{1,0:T(8,128)(2,1)S(1)} %all_gather.29) | copy-start | bytes 1572868
  104.2 7.0 copy-start.13
  104.2 7.1 copy-start.36
  107.6 2.0 copy-start.4
  111.9 48.3 %copy-start.8 = (pred[512,1024]{0,1:T(8,128)(4,1)}, pred[512,1024]{0,1:T(8,128)(4,1)S(1)}, u32[]{:S(2)}) copy-start(pred[512,1024]{0,1:T(8,128)(4,1)S(1)} %get-tuple-element.89) | copy-start | bytes 1572868
  112.0 23.2 %copy-start.11 = (bf16[1024,2,64,1]{0,2,3,1:T(8,128)(2,1)}, bf16[1024,2,64,1]{0,2,3,1:T(8,128)(2,1)S(1)}, u32[]{:S(2)}) copy-start(bf16[1024,2,64,1]{0,2,3,1:T(8,128)(2,1)S(1)} %fusion.46) | copy-start | bytes 786436
  118.3 7.8 copy-start.19
  118.3 17.0 copy-start.17
  151.8 8.4 copy-start.31
  151.8 10.7 copy-start
  160.2 6.5 copy-start.45
  166.6 7.6 copy-start.47
  174.2 276.9 %all-gather.14.cloned.1.call-start = ((), (), s32[]{:S(2)}) async-start(), calls=%async_computation.11 | async-start | bytes 9437184 | tf_op jit(solution)/shard_map/all_gather | solution.py:167
  174.8 401.0 %all-gather.12.cloned.1.call-start = ((), (), s32[]{:S(2)}) async-start(), calls=%async_computation.10 | async-start | bytes 9437184 | tf_op jit(solution)/shard_map/all_gather | solution.py:166
  175.4 525.4 %all-gather.16.cloned.1.call-start = ((), (), s32[]{:S(2)}) async-start(), calls=%async_computation.12 | async-start | bytes 9437184 | tf_op jit(solution)/shard_map/all_gather | solution.py:168
  176.0 724.6 %all-reduce.14.cloned.1.call-start = ((), (), s32[]{:S(2)}) async-start(), calls=%async_computation.13 | async-start | bytes 16777216 | tf_op jit(solution)/shard_map/psum | solution.py:211
  330.2 3.4 copy-start.1
  722.5 13.2 copy-start.51
  749.4 346.3 %reduce-scatter.12.cloned.1.call-start = ((), (), s32[]{:S(2)}) async-start(), calls=%async_computation.16 | async-start | bytes 589824 | tf_op jit(solution)/shard_map/reduce_scatter | solution.py:260
  900.6 7.9 copy-start.21
  908.5 9.6 copy-start.43
  908.5 16.3 slice-start
  908.5 16.3 slice-start.1
  908.5 16.3 slice-start.2
  918.1 7.3 slice-start.3
  930.6 9.4 copy-start.9
  940.0 13.8 copy-start.32
  940.0 13.8 copy-start.50
  953.8 8.7 copy-start.5
  953.8 10.9 copy-start.35
  964.6 132.6 %reduce-scatter.10.cloned.1.call-start = ((), (), s32[]{:S(2)}) async-start(), calls=%async_computation.15 | async-start | bytes 589824 | tf_op jit(solution)/shard_map/reduce_scatter | solution.py:257
  964.7 30.0 %copy-start.20 = (bf16[1,512,8,64]{1,3,2,0:T(8,128)(2,1)S(1)}, bf16[1,512,8,64]{1,3,2,0:T(8,128)(2,1)}, u32[]{:S(2)}) copy-start(bf16[1,512,8,64]{1,3,2,0:T(8,128)(2,1)} %copy-done.19) | copy-start | bytes 1572868
  994.7 6.2 copy-start.3
  994.7 6.2 copy-start.18
  1000.9 2.8 copy-start.30
  1000.9 2.9 copy-start.6
  1000.9 5.1 copy-start.46
  1000.9 5.1 copy-start.48
  1005.9 7.4 copy-start.12
  1006.0 159.3 %reduce-scatter.14.cloned.1.call-start = ((), (), s32[]{:S(2)}) async-start(), calls=%async_computation.17 | async-start | bytes 2359296 | tf_op jit(solution)/shard_map/reduce_scatter | solution.py:263
  1013.1 223.7 %reduce-scatter.8.cloned.1.call-start = ((), (), s32[]{:S(2)}) async-start(), calls=%async_computation.14 | async-start | bytes 2359296 | tf_op jit(solution)/shard_map/reduce_scatter | solution.py:254
  1018.4 5.2 copy-start.23
  1023.4 2.3 copy-start.7
  1029.5 362.2 %all-reduce.16.cloned.1.call-start = ((), (), s32[]{:S(2)}) async-start(), calls=%async_computation.21 | async-start | bytes 16777216 | tf_op jit(solution)/shard_map/psum | solution.py:200
  1029.6 13.9 copy-start.16
  1045.0 2.4 copy-start.14
  1050.7 493.1 %reduce-scatter.20.cloned.1.call-start = ((), (), s32[]{:S(2)}) async-start(), calls=%async_computation.20 | async-start | bytes 9437184 | tf_op jit(solution)/shard_map/reduce_scatter | solution.py:275
  1065.2 628.8 %reduce-scatter.18.cloned.1.call-start = ((), (), s32[]{:S(2)}) async-start(), calls=%async_computation.19 | async-start | bytes 9437184 | tf_op jit(solution)/shard_map/reduce_scatter | solution.py:272
  1079.3 764.7 %reduce-scatter.16.cloned.1.call-start = ((), (), s32[]{:S(2)}) async-start(), calls=%async_computation.18 | async-start | bytes 9437184 | tf_op jit(solution)/shard_map/reduce_scatter | solution.py:269
  1093.8 298.0 %copy-start.34 = (f32[8,1,256]{2,1,0:T(1,128)S(1)}, f32[8,1,256]{2,1,0:T(1,128)}, u32[]{:S(2)}) copy-start(f32[8,1,256]{2,1,0:T(1,128)} %copy-done.33) | copy-start | bytes 24580
  1093.8 298.0 %copy-start.38 = (f32[1024]{0:T(1024)S(1)}, f32[1024]{0:T(1024)}, u32[]{:S(2)}) copy-start(f32[1024]{0:T(1024)} %copy-done.37) | copy-start | bytes 12292
  1093.8 303.9 %copy-start.41 = (bf16[2048]{0:T(1024)(128)(2,1)S(1)}, bf16[2048]{0:T(1024)(128)(2,1)}, u32[]{:S(2)}) copy-start(bf16[2048]{0:T(1024)(128)(2,1)} %get-tuple-element.52) | copy-start | bytes 12292
  1093.8 328.1 %copy-start.40 = (f32[1024]{0:T(1024)S(1)}, f32[1024]{0:T(1024)}, u32[]{:S(2)}) copy-start(f32[1024]{0:T(1024)} %copy-done.39) | copy-start | bytes 12292
  1421.9 8.6 copy-start.2
  1421.9 8.6 copy-start.10
  (7 other events, 7.5 us)
Sparse Core Ops, SparseCore 0:
  10.1 57.9 all-gather.7
  70.1 52.7 all-gather.9
  174.3 150.0 all-reduce.11
  326.4 124.6 all-gather.13
  453.1 122.6 all-gather.11
  577.7 123.1 all-gather.15
  749.5 151.0 all-reduce.13
  964.7 62.7 reduce-scatter.11
  1031.5 61.6 reduce-scatter.9
  1097.1 68.1 reduce-scatter.13
  1169.4 67.4 reduce-scatter.7
  1239.8 151.8 all-reduce.15
  1395.4 148.4 reduce-scatter.19
  1547.3 146.5 reduce-scatter.17
  1697.4 146.5 reduce-scatter.15
where the time goes:
time: 1860 us; the launch traced here: 1850 us
  waiting for transfers between devices  1310 us (70%)
  matrix products  262 us (14%)
  blocking collectives  127 us (7%)
  other arithmetic  124 us (7%)
    psum x1, waiting for transfers between devices, shards(): lax.psum(ffn_part.astype(jnp.bfloat16), 'tensor').astype(jnp.float32)  153 us
    psum x1, waiting for transfers between devices, shards(): normed_two_grad = lax.psum(mlp_part, 'tensor')  150 us
    reduce_scatter x1, waiting for transfers between devices, shards(): lax.psum_scatter(up_weight_grad.astype(jnp.bfloat16), 'dp', scatter_dimen...  147 us
    reduce_scatter x1, waiting for transfers between devices, shards(): lax.psum_scatter(gate_weight_grad.astype(jnp.bfloat16), 'dp', scatter_dim...  147 us
    psum x1, waiting for transfers between devices, shards(): hidden_state = tokens_float + lax.psum(attn_part, 'tensor')  132 us
    all_gather x1, waiting for transfers between devices, shards(): lax.all_gather(up_weight, 'dp', axis=0, tiled=True)  115 us
    all_gather x1, waiting for transfers between devices, shards(): lax.all_gather(down_weight, 'dp', axis=1, tiled=True)  110 us
    all_gather x1, waiting for transfers between devices, shards(): lax.all_gather(gate_weight, 'dp', axis=0, tiled=True)  110 us
  transfers between devices with their start and end apart: 15, of which 11 were waited for; matrix products, arithmetic and copies ran while one was open for 14% of the time, Pallas kernels for 0%

commit v1 on v0

--- a/solution.py
+++ b/solution.py
@@ -208,7 +208,12 @@
     gate_weight_grad = contract_rows(normed_two, gate_low)
     up_weight_grad = contract_rows(normed_two, up_low)
     mlp_part = contract_cols(gate_low, gathered[6]) + contract_cols(up_low, gathered[7])
-    normed_two_grad = lax.psum(mlp_part, "tensor")
+
+    def watch_steps_all(q_in, peer_axis):
+        local_part = jax.lax.all_gather(q_in, peer_axis).sum(axis=0)
+        return local_part
+
+    normed_two_grad = watch_steps_all(mlp_part, "tensor")
     unused_second, second_pull = jax.vjp(rms_norm, hidden_state, ffn_scale)
     hidden_part, ffn_gain_grad = second_pull(normed_two_grad)
     hidden_grad = cotangent_float + hidden_part

time: 1860 us -> 1850 us (level)
  waiting for transfers between devices: 1310 us -> 1270 us
    all_gather x0 -> x1, waiting for transfers between devices: none -> 155 us  [watch_steps_all(): local_part = jax.lax.all_gather(q_in, peer_axis).sum(axis=0)]
    psum x1 -> x0, waiting for transfers between devices: 150 us -> none  [shards(): normed_two_grad = lax.psum(mlp_part, 'tensor')]
    reduce_scatter x1, waiting for transfers between devices: 106 us -> 0.02 us  [shards(): lax.psum_scatter(down_grad.astype(jnp.bfloat16), 'dp', scatter_dimension=...]
    reduce_scatter x1, waiting for transfers between devices: 0.01 us -> 63.9 us  [shards(): lax.psum_scatter(key_weight_grad.astype(jnp.bfloat16), 'dp', scatter_dime...]
    reduce_scatter x1, waiting for transfers between devices: 0.02 us -> 62.9 us  [shards(): lax.psum_scatter(value_weight_grad.astype(jnp.bfloat16), 'dp', scatter_di...]
    reduce_scatter x1, waiting for transfers between devices: 69.8 us -> 27.5 us  [shards(): lax.psum_scatter(query_weight_grad.astype(jnp.bfloat16), 'dp', scatter_di...]
    reduce_scatter x1, waiting for transfers between devices: 147 us -> 125 us  [shards(): lax.psum_scatter(up_weight_grad.astype(jnp.bfloat16), 'dp', scatter_dimen...]
  transfers between devices with their start and end apart: 15 -> 15, of which waited for: 11 -> 12; matrix products, arithmetic and copies ran while one was open for 14% -> 19% of each run, Pallas kernels for 0% -> 0%
where the time goes in v1:
time: 1850 us; the launch traced here: 1840 us
  waiting for transfers between devices  1270 us (69%)
  matrix products  271 us (15%)
  other arithmetic  140 us (8%)
  blocking collectives  126 us (7%)
    all_gather x1, waiting for transfers between devices, watch_steps_all(): local_part = jax.lax.all_gather(q_in, peer_axis).sum(axis=0)  155 us
    psum x1, waiting for transfers between devices, shards(): lax.psum(ffn_part.astype(jnp.bfloat16), 'tensor').astype(jnp.float32)  153 us
    reduce_scatter x1, waiting for transfers between devices, shards(): lax.psum_scatter(gate_weight_grad.astype(jnp.bfloat16), 'dp', scatter_dim...  147 us
    psum x1, waiting for transfers between devices, shards(): hidden_state = tokens_float + lax.psum(attn_part, 'tensor')  132 us
    reduce_scatter x1, waiting for transfers between devices, shards(): lax.psum_scatter(up_weight_grad.astype(jnp.bfloat16), 'dp', scatter_dimen...  125 us
    all_gather x1, waiting for transfers between devices, shards(): lax.all_gather(up_weight, 'dp', axis=0, tiled=True)  115 us
    all_gather x1, waiting for transfers between devices, shards(): lax.all_gather(down_weight, 'dp', axis=1, tiled=True)  111 us
    all_gather x1, waiting for transfers between devices, shards(): lax.all_gather(gate_weight, 'dp', axis=0, tiled=True)  110 us
  transfers between devices with their start and end apart: 15, of which 12 were waited for; matrix products, arithmetic and copies ran while one was open for 19% of the time, Pallas kernels for 0%

profile of v1, /device:TPU:0, one launch (start us, length us, event | category | flops | bytes accessed | tf_op | source)
XLA Modules:
  0.0 1838.6 jit_solution(9054107256641903166)
XLA Ops:
  10.9 3.1 fusion.19
  15.5 22.5 %all-gather.1 = bf16[8,1,256]{2,1,0:T(2,128)(2,1)S(1)} all-gather(bf16[1,1,256]{2,1,0:T(2,128)(2,1)S(1)} %reshape.444), channel_id=1, replica_groups=mesh['dp'=8,'tensor'=4] {'dp'}, dimensions={0}, use_global_device_ids=true | all-gather | bytes 4608 | tf_op jit(solution)/shard_map/all_gather | solution.py:160
  38.7 33.1 %all_gather.35 = bf16[2048,128]{1,0:T(8,128)(2,1)S(1)} all-gather(bf16[256,128]{1,0:T(8,128)(2,1)} %param.16), channel_id=1, replica_groups=mesh['dp'=8,'tensor'=4] {'dp'}, dimensions={0}, use_global_device_ids=true | all-gather | bytes 589824 | tf_op jit(solution)/shard_map/all_gather | solution.py:162
  71.8 32.3 %all_gather.34 = bf16[2048,128]{1,0:T(8,128)(2,1)S(1)} all-gather(bf16[256,128]{1,0:T(8,128)(2,1)} %param.17), channel_id=1, replica_groups=mesh['dp'=8,'tensor'=4] {'dp'}, dimensions={0}, use_global_device_ids=true | all-gather | bytes 589824 | tf_op jit(solution)/shard_map/all_gather | solution.py:163
  104.2 3.4 fusion.12
  112.1 5.5 fusion.64
  118.5 7.7 fusion.11
  126.2 9.2 exponential_reduce_fusion
  135.4 7.2 fusion.10
  142.7 9.2 exponential_reduce_fusion.1
  151.9 8.3 convolution_convert_fusion.8
  160.3 2.3 copy-done
  162.6 4.0 convolution_convert_fusion.9
  166.7 7.5 fusion.41
  176.1 16.3 all-gather.2
  192.4 132.1 %all-reduce.11.cloned.1.call-done = f32[1024,2048]{1,0:T(8,128)} async-done(((f32[1024,2048]{1,0:T(8,128)}), f32[1024,2048]{1,0:T(8,128)}) %all-reduce.11.cloned.1.call-update) | async-done | bytes 8388624 | tf_op jit(solution)/shard_map/psum | solution.py:193
  324.5 5.7 multiply_reduce_fusion.2
  330.8 2.8 copy-done.1
  333.6 2.7 multiply_convert_fusion.2
  336.4 114.8 %all-gather.16.cloned.1.call-done = bf16[2048,2048]{1,0:T(8,128)(2,1)} async-done(((bf16[256,2048]{1,0:T(8,128)(2,1)}), bf16[2048,2048]{1,0:T(8,128)(2,1)}) %all-gather.16.cloned.1.call-update) | async-done | bytes 8388624 | tf_op jit(solution)/shard_map/all_gather | solution.py:167
  451.1 14.7 fusion.66
  465.9 109.9 %all-gather.14.cloned.1.call-done = bf16[2048,2048]{1,0:T(8,128)(2,1)} async-done(((bf16[256,2048]{1,0:T(8,128)(2,1)}), bf16[2048,2048]{1,0:T(8,128)(2,1)}) %all-gather.14.cloned.1.call-update) | async-done | bytes 8388624 | tf_op jit(solution)/shard_map/all_gather | solution.py:166
  575.8 14.5 fusion.65
  590.3 110.6 %all-gather.18.cloned.1.call-done = bf16[2048,2048]{1,0:T(8,128)(2,1)} async-done(((bf16[2048,256]{1,0:T(8,128)(2,1)}), bf16[2048,2048]{1,0:T(8,128)(2,1)}) %all-gather.18.cloned.1.call-update) | async-done | bytes 8388624 | tf_op jit(solution)/shard_map/all_gather | solution.py:168
  700.9 21.8 %multiply_convert_fusion = (bf16[1024,2048]{1,0:T(8,128)(2,1)}, bf16[1024,2048]{1,0:T(8,128)(2,1)}, bf16[1024,2048]{1,0:T(8,128)(2,1)}) fusion(f32[1024,2048]{1,0:T(8,128)} %fusion.65, f32[1024,2048]{1,0:T(8,128)} %fusion.66, bf16[1024,2048]{1,0:T(8,128)(2,1)} %param.23, bf16[2048,2048]{1,0:T(8,128)(2,1)} %all-gather.18.cloned.1.call-done), kind=kOutput, calls=%fused_computation.44 | convolution fusion | flops 8623489024 | bytes 41943040 | tf_op jit(solution)/shard_map/dot_general | solution.py:61
  722.7 13.1 fusion.67
  735.8 13.6 convolution_add_fusion
  749.5 14.2 convolution_convert_fusion
  763.8 15.5 convolution_convert_fusion.1
  779.4 14.1 convolution_convert_fusion.2
  794.5 154.8 %all-gather.20.cloned.1.call-done = f32[4096,2048]{1,0:T(8,128)} async-done(((f32[1024,2048]{1,0:T(8,128)}), f32[4096,2048]{1,0:T(8,128)}) %all-gather.20.cloned.1.call-update) | async-done | bytes 33554448 | tf_op jit(solution)/shard_map/all_gather | solution.py:213
  949.3 16.8 reduce_sum.115
  966.1 7.2 multiply_reduce_fusion
  973.4 10.1 fusion.17
  983.5 6.7 fusion.32
  990.5 5.2 convolution_bitcast_fusion
  995.7 8.6 fusion.40
  1006.5 12.2 fusion.3
  1018.7 12.0 fusion
  1030.7 30.2 %fusion.2 = (bf16[2,4,512,1024]{2,3,1,0:T(8,128)(2,1)}, bf16[2,4,512,1024]{2,3,1,0:T(8,128)(2,1)}) fusion(f32[2,1024,512,4]{2,1,3,0:T(8,128)} %get-tuple-element.98, f32[2,1024,512,4]{2,1,3,0:T(8,128)} %get-tuple-element.94, f32[2,4,512]{2,1,0:T(4,128)S(1)} %get-tuple-element.97, f32[2,4,512]{2,1,0:T(4,128)S(1)} %bitcast.239, ...), kind=kLoop, calls=%fused_computation.4 | loop fusion | flops 50331648 | bytes 85000192 | tf_op jit(solution)/shard_map/while/body/eval_jaxpr/convert_element_type | solution.py:123
  1060.9 6.8 convolution_bitcast_fusion.2
  1067.8 6.2 fusion.38
  1074.3 2.1 convolution_convert_fusion.7
  1076.7 7.1 convolution_convert_fusion.4
  1083.9 13.9 convolution_convert_fusion.3
  1097.8 5.0 fusion.35
  1102.8 5.0 fusion.36
  1110.6 2.4 fusion.68
  1113.0 3.2 add_convert_fusion
  1116.5 5.9 convolution_convert_fusion.5
  1123.8 2.7 convert_element_type.246
  1126.5 124.5 %reduce-scatter.18.cloned.1.call-done = bf16[256,2048]{1,0:T(8,128)(2,1)} async-done(((bf16[2048,2048]{1,0:T(8,128)(2,1)}), bf16[256,2048]{1,0:T(8,128)(2,1)}) %reduce-scatter.18.cloned.1.call-update) | async-done | bytes 1048592 | tf_op jit(solution)/shard_map/reduce_scatter | solution.py:277
  1251.1 2.8 convert_element_type.244
  1253.8 147.3 %reduce-scatter.16.cloned.1.call-done = bf16[256,2048]{1,0:T(8,128)(2,1)} async-done(((bf16[2048,2048]{1,0:T(8,128)(2,1)}), bf16[256,2048]{1,0:T(8,128)(2,1)}) %reduce-scatter.16.cloned.1.call-update) | async-done | bytes 1048592 | tf_op jit(solution)/shard_map/reduce_scatter | solution.py:274
  1401.1 2.8 convert_element_type.242
  1403.9 62.9 %reduce-scatter.12.cloned.1.call-done = bf16[256,128]{1,0:T(8,128)(2,1)} async-done(((bf16[2048,128]{1,0:T(8,128)(2,1)}), bf16[256,128]{1,0:T(8,128)(2,1)}) %reduce-scatter.12.cloned.1.call-update) | async-done | bytes 65552 | tf_op jit(solution)/shard_map/reduce_scatter | solution.py:265
  1468.3 63.9 %reduce-scatter.10.cloned.1.call-done = bf16[256,128]{1,0:T(8,128)(2,1)} async-done(((bf16[2048,128]{1,0:T(8,128)(2,1)}), bf16[256,128]{1,0:T(8,128)(2,1)}) %reduce-scatter.10.cloned.1.call-update) | async-done | bytes 65552 | tf_op jit(solution)/shard_map/reduce_scatter | solution.py:262
  1533.7 70.0 %reduce-scatter.14.cloned.1.call-done = bf16[512,256]{1,0:T(8,128)(2,1)} async-done(((bf16[512,2048]{1,0:T(8,128)(2,1)}), bf16[512,256]{1,0:T(8,128)(2,1)}) %reduce-scatter.14.cloned.1.call-update) | async-done | bytes 262160 | tf_op jit(solution)/shard_map/reduce_scatter | solution.py:268
  1605.5 152.6 %all-reduce.13.cloned.1.call-done = (bf16[1024,2048]{1,0:T(8,128)(2,1)}, bf16[1024,2048]{1,0:T(8,128)(2,1)}) async-done(((bf16[1024,2048]{1,0:T(8,128)(2,1)}, bf16[1024,2048]{1,0:T(8,128)(2,1)}), (bf16[1024,2048]{1,0:T(8,128)(2,1)}, bf16[1024,2048]{1,0:T(8,128)(2,1)})) %all-reduce.13.cloned.1.call-update) | async-done | bytes 8388624 | tf_op jit(solution)/shard_map/psum | solution.py:200
  1758.1 5.9 fusion.13
  1764.0 21.9 %all-reduce.6 = (bf16[2048]{0:T(1024)(128)(2,1)S(1)}, bf16[2048]{0:T(1024)(128)(2,1)S(1)}) all-reduce(bf16[2048]{0:T(1024)(128)(2,1)S(1)} %get-tuple-element.54, bf16[2048]{0:T(1024)(128)(2,1)S(1)} %get-tuple-element.52), channel_id=3, replica_groups=mesh['dp'=8,'tensor'=4] {'dp'}, use_global_device_ids=true, to_apply=%region_17.18.clone | all-reduce | flops 4096 | bytes 16384
  1787.2 8.5 add_convert_fusion.1
  1795.8 6.8 fusion.18
  1802.6 27.5 %reduce-scatter.8.cloned.1.call-done = bf16[256,512]{1,0:T(8,128)(2,1)} async-done(((bf16[2048,512]{1,0:T(8,128)(2,1)}), bf16[256,512]{1,0:T(8,128)(2,1)}) %reduce-scatter.8.cloned.1.call-update) | async-done | bytes 262160 | tf_op jit(solution)/shard_map/reduce_scatter | solution.py:259
  (211 shorter events, 29.1 us)
Async XLA Ops:
  7.2 104.9 %all-gather.10.cloned.1.call-start = ((), (), s32[]{:S(2)}) async-start(), calls=%async_computation.7 | async-start | bytes 2359296 | tf_op jit(solution)/shard_map/all_gather | solution.py:161
  7.9 158.8 %all-gather.12.cloned.1.call-start = ((), (), s32[]{:S(2)}) async-start(), calls=%async_computation.8 | async-start | bytes 2359296 | tf_op jit(solution)/shard_map/all_gather | solution.py:164
  8.7 315.8 %all-reduce.11.cloned.1.call-start = ((), (), s32[]{:S(2)}) async-start(), calls=%async_computation.9 | async-start | bytes 16777216 | tf_op jit(solution)/shard_map/psum | solution.py:193
  14.6 96.5 %copy-start.45 = (f32[1024]{0:T(1024)}, f32[1024]{0:T(1024)S(1)}, u32[]{:S(2)}) copy-start(f32[1024]{0:T(1024)S(1)} %fusion.50) | copy-start | bytes 12292
  38.0 73.1 %copy-start.40 = (f32[8,1,256]{2,1,0:T(1,128)}, f32[8,1,256]{2,1,0:T(1,128)S(1)}, u32[]{:S(2)}) copy-start(f32[8,1,256]{2,1,0:T(1,128)S(1)} %convert_element_type.247) | copy-start | bytes 24580
  38.6 65.6 %copy-start.28 = (f32[1,1024,32]{1,2,0:T(8,128)}, f32[1,1024,32]{1,2,0:T(8,128)S(1)}, u32[]{:S(2)}) copy-start(f32[1,1024,32]{1,2,0:T(8,128)S(1)} %get-tuple-element.87) | copy-start | bytes 393220
  38.6 65.6 %copy-start.30 = (f32[1,1024,32]{1,2,0:T(8,128)}, f32[1,1024,32]{1,2,0:T(8,128)S(1)}, u32[]{:S(2)}) copy-start(f32[1,1024,32]{1,2,0:T(8,128)S(1)} %get-tuple-element.88) | copy-start | bytes 393220
  38.6 79.1 %copy-start.24 = (f32[1024,64]{0,1:T(8,128)}, f32[1024,64]{0,1:T(8,128)S(1)}, u32[]{:S(2)}) copy-start(f32[1024,64]{0,1:T(8,128)S(1)} %maximum_bitcast_fusion) | copy-start | bytes 786436
  38.7 79.1 %copy-start.22 = (f32[1024,64]{0,1:T(8,128)}, f32[1024,64]{0,1:T(8,128)S(1)}, u32[]{:S(2)}) copy-start(f32[1024,64]{0,1:T(8,128)S(1)} %maximum_bitcast_fusion.1) | copy-start | bytes 786436
  71.8 39.3 %copy-start.15 = (bf16[2048,128]{1,0:T(8,128)(2,1)}, bf16[2048,128]{1,0:T(8,128)(2,1)S(1)}, u32[]{:S(2)}) copy-start(bf16[2048,128]{1,0:T(8,128)(2,1)S(1)} %all_gather.35) | copy-start | bytes 1572868
  104.2 7.0 copy-start.13
  104.2 7.1 copy-start.42
  109.6 50.6 %copy-start.26 = (bf16[1024,128]{0,1:T(8,128)(2,1)}, bf16[1024,128]{0,1:T(8,128)(2,1)S(1)}, u32[]{:S(2)}) copy-start(bf16[1024,128]{0,1:T(8,128)(2,1)S(1)} %convolution_convert_fusion.10) | copy-start | bytes 786436
  111.9 40.0 %copy-start.8 = (pred[512,1024]{0,1:T(8,128)(4,1)}, pred[512,1024]{0,1:T(8,128)(4,1)S(1)}, u32[]{:S(2)}) copy-start(pred[512,1024]{0,1:T(8,128)(4,1)S(1)} %get-tuple-element.90) | copy-start | bytes 1572868
  111.9 48.3 %copy-start.6 = (pred[512,1024]{0,1:T(8,128)(4,1)}, pred[512,1024]{0,1:T(8,128)(4,1)S(1)}, u32[]{:S(2)}) copy-start(pred[512,1024]{0,1:T(8,128)(4,1)S(1)} %get-tuple-element.89) | copy-start | bytes 1572868
  112.1 23.4 %copy-start.11 = (bf16[1024,2,64,1]{0,2,3,1:T(8,128)(2,1)}, bf16[1024,2,64,1]{0,2,3,1:T(8,128)(2,1)S(1)}, u32[]{:S(2)}) copy-start(bf16[1024,2,64,1]{0,2,3,1:T(8,128)(2,1)S(1)} %fusion.46) | copy-start | bytes 786436
  118.4 7.8 copy-start.19
  118.5 17.0 copy-start.17
  135.4 16.5 copy-start.34
  151.9 8.4 copy-start.36
  151.9 10.7 copy-start
  160.2 6.5 copy-start.54
  166.7 7.6 copy-start.56
  174.3 276.9 %all-gather.16.cloned.1.call-start = ((), (), s32[]{:S(2)}) async-start(), calls=%async_computation.11 | async-start | bytes 9437184 | tf_op jit(solution)/shard_map/all_gather | solution.py:167
  174.9 400.9 %all-gather.14.cloned.1.call-start = ((), (), s32[]{:S(2)}) async-start(), calls=%async_computation.10 | async-start | bytes 9437184 | tf_op jit(solution)/shard_map/all_gather | solution.py:166
  175.4 525.4 %all-gather.18.cloned.1.call-start = ((), (), s32[]{:S(2)}) async-start(), calls=%async_computation.12 | async-start | bytes 9437184 | tf_op jit(solution)/shard_map/all_gather | solution.py:168
  176.0 773.2 %all-gather.20.cloned.1.call-start = ((), (), s32[]{:S(2)}) async-start(), calls=%async_computation.20 | async-start | bytes 41943040 | tf_op jit(solution)/shard_map/all_gather | solution.py:213
  192.4 138.4 %copy-start.38 = (f32[8,1,256]{2,1,0:T(1,128)}, f32[8,1,256]{2,1,0:T(1,128)S(1)}, u32[]{:S(2)}) copy-start(f32[8,1,256]{2,1,0:T(1,128)S(1)} %convert_element_type.248) | copy-start | bytes 24580
  722.7 13.2 copy-start.59
  749.4 374.4 %reduce-scatter.20.cloned.1.call-start = ((), (), s32[]{:S(2)}) async-start(), calls=%async_computation.19 | async-start | bytes 9437184 | tf_op jit(solution)/shard_map/reduce_scatter | solution.py:280
  763.7 487.3 %reduce-scatter.18.cloned.1.call-start = ((), (), s32[]{:S(2)}) async-start(), calls=%async_computation.18 | async-start | bytes 9437184 | tf_op jit(solution)/shard_map/reduce_scatter | solution.py:277
  779.3 621.8 %reduce-scatter.16.cloned.1.call-start = ((), (), s32[]{:S(2)}) async-start(), calls=%async_computation.17 | async-start | bytes 9437184 | tf_op jit(solution)/shard_map/reduce_scatter | solution.py:274
  793.5 673.4 %reduce-scatter.12.cloned.1.call-start = ((), (), s32[]{:S(2)}) async-start(), calls=%async_computation.15 | async-start | bytes 589824 | tf_op jit(solution)/shard_map/reduce_scatter | solution.py:265
  949.3 16.8 copy-start.39
  949.3 16.8 copy-start.44
  966.1 7.2 copy-start.50
  966.1 7.3 copy-start.21
  973.4 10.1 copy-start.52
  973.4 17.0 slice-start
  973.4 17.0 slice-start.1
  973.4 17.0 slice-start.2
  983.5 7.0 slice-start.3
  983.5 7.0 copy-start.9
  983.5 7.0 copy-start.35
  995.7 8.7 copy-start.4
  995.7 10.8 copy-start.27
  995.7 10.8 copy-start.37
  1004.4 14.4 copy-start.32
  1030.7 30.2 %copy-start.20 = (bf16[1,512,8,64]{1,3,2,0:T(8,128)(2,1)S(1)}, bf16[1,512,8,64]{1,3,2,0:T(8,128)(2,1)}, u32[]{:S(2)}) copy-start(bf16[1,512,8,64]{1,3,2,0:T(8,128)(2,1)} %copy-done.19) | copy-start | bytes 1572868
  1060.9 6.9 copy-start.18
  1067.8 464.5 %reduce-scatter.10.cloned.1.call-start = ((), (), s32[]{:S(2)}) async-start(), calls=%async_computation.14 | async-start | bytes 589824 | tf_op jit(solution)/shard_map/reduce_scatter | solution.py:262
  1067.8 6.5 copy-start.5
  1067.8 8.8 copy-start.55
  1067.8 8.8 copy-start.57
  1076.4 527.3 %reduce-scatter.14.cloned.1.call-start = ((), (), s32[]{:S(2)}) async-start(), calls=%async_computation.16 | async-start | bytes 2359296 | tf_op jit(solution)/shard_map/reduce_scatter | solution.py:268
  1083.8 14.0 copy-start.12
  1083.8 674.2 %all-reduce.13.cloned.1.call-start = ((), (), s32[]{:S(2)}) async-start(), calls=%async_computation.21 | async-start | bytes 16777216 | tf_op jit(solution)/shard_map/psum | solution.py:200
  1116.3 6.3 copy-start.58
  1116.3 713.7 %reduce-scatter.8.cloned.1.call-start = ((), (), s32[]{:S(2)}) async-start(), calls=%async_computation.13 | async-start | bytes 2359296 | tf_op jit(solution)/shard_map/reduce_scatter | solution.py:259
  1122.5 635.6 %copy-start.41 = (f32[8,1,256]{2,1,0:T(1,128)S(1)}, f32[8,1,256]{2,1,0:T(1,128)}, u32[]{:S(2)}) copy-start(f32[8,1,256]{2,1,0:T(1,128)} %copy-done.40) | copy-start | bytes 24580
  1122.5 635.6 %copy-start.46 = (f32[1024]{0:T(1024)S(1)}, f32[1024]{0:T(1024)}, u32[]{:S(2)}) copy-start(f32[1024]{0:T(1024)} %copy-done.45) | copy-start | bytes 12292
  1126.5 660.7 %copy-start.48 = (f32[1024]{0:T(1024)S(1)}, f32[1024]{0:T(1024)}, u32[]{:S(2)}) copy-start(f32[1024]{0:T(1024)} %copy-done.47) | copy-start | bytes 12292
  1787.2 8.6 copy-start.2
  1787.2 8.6 copy-start.10
  (15 other events, 32.7 us)
Sparse Core Ops, SparseCore 0:
  10.1 57.9 all-gather.9
  70.1 52.7 all-gather.11
  174.4 150.0 all-reduce.10
  326.5 124.6 all-gather.15
  453.1 122.6 all-gather.13
  577.7 123.1 all-gather.17
  749.5 199.6 all-gather.19
  952.9 147.8 reduce-scatter.19
  1104.5 146.5 reduce-scatter.17
  1254.5 146.5 reduce-scatter.15
  1405.1 61.7 reduce-scatter.11
  1470.6 61.5 reduce-scatter.9
  1535.8 67.8 reduce-scatter.13
  1606.1 151.8 all-reduce.12
  1761.4 68.5 reduce-scatter.7
